TPU v7x, 32 devices: a whole 2x2x4 slice. The times are simulated.
32 devices in a mesh: wide: 8 (over y, x, core), narrow: 4 (over z).
Axes of the slice: x: 2, y: 2, z: 4, core: 2. Of those that a mesh axis runs over, the one named last changes fastest.
Arguments:
- hidden_in: bfloat16 [4096, 1536], P('wide'), may hold values from -64 to 64
- segment_ids: int32 [4096], P('wide'), may hold values from 0 to 7, as said below
- seg_lengths: int32 [8], replicated, may hold values from 1 to 2048, as said below
- seg_offsets: int32 [8], replicated, may hold values from 0 to 4095, as said below
- block_table: int32 [8, 16], replicated, may hold values from -1 to 39, as said below
- attn_gain: bfloat16 [1536], replicated, may hold values from 0.099609375 to 1.8984375
- w_query: bfloat16 [1536, 1536], P('wide', 'narrow'), may hold values from -0.15625 to 0.15625
- b_query: bfloat16 [1536], P('narrow'), may hold values from -128 to 128
- w_keyval: bfloat16 [1536, 512], P('wide'), may hold values from -0.15625 to 0.15625
- b_keyval: bfloat16 [512], replicated, may hold values from -128 to 128
- w_out: bfloat16 [1536, 1536], P('narrow', 'wide'), may hold values from -0.15625 to 0.15625
- mlp_gain: bfloat16 [1536], replicated, may hold values from 0.099609375 to 1.8984375
- w_gate: bfloat16 [1536, 8960], P('wide', 'narrow'), may hold values from -0.15625 to 0.15625
- w_up: bfloat16 [1536, 8960], P('wide', 'narrow'), may hold values from -0.15625 to 0.15625
- w_down: bfloat16 [8960, 1536], P('narrow', 'wide'), may hold values from -0.0625 to 0.0625
- next_gain: bfloat16 [1536], replicated, may hold values from 0.099609375 to 1.8984375
- w_query2: bfloat16 [1536, 1536], P('wide', 'narrow'), may hold values from -0.15625 to 0.15625
- b_query2: bfloat16 [1536], P('narrow'), may hold values from -3 to 3
- w_keyval2: bfloat16 [1536, 512], P('wide'), may hold values from -0.15625 to 0.15625
- b_keyval2: bfloat16 [512], replicated, may hold values from -3 to 3
Outputs:
- hidden_out: bfloat16 [4096, 1536], P('wide')
- next_query: bfloat16 [4096, 1536], P('wide', 'narrow')
- next_keyval: bfloat16 [4096, 512], P('wide', 'narrow')
- kv_cache: bfloat16 [4, 40, 128, 128], P('narrow', 'wide')
Inputs may be any that keep to these rules, and one draw needn't show every extreme that they name: `segment_ids`: segment s covers tokens seg_offsets[s] to seg_offsets[s] + seg_lengths[s] - 1. `seg_lengths`: they sum to 4096. seg_offsets[0] = 0 and seg_offsets[s + 1] = seg_offsets[s] + seg_lengths[s]. `block_table`: entry j of row s is a page for j below ceil(seg_lengths[s] / 128) and -1 beyond; no page appears twice.
All inputs are finite; a program needn't handle non-finite values.
Results may differ from a plain program's by a relative error of at most 0.017.
Values may be sent and summed in bfloat16 or wider, within the bound.
No kernel may reach another device: no remote copies, remote signals or barrier semaphores. Data moves between devices by JAX's collectives and lax.ppermute only.
A program may use at most 128 MiB of HBM per device.

v0:
```python
import math
import jax
import jax.numpy as jnp
from jax import lax
from jax.sharding import PartitionSpec as P

HD = 128
PAGE_LEN = 128
norm_eps = 1e-06
rope_base = 1000000.0
masked_score = -1e30


def rms_norm(activations, gain_vector):
    values = activations.astype(jnp.float32)
    row_scale = lax.rsqrt(jnp.mean(values * values, axis=-1, keepdims=True) + norm_eps)
    return (values * row_scale * gain_vector.astype(jnp.float32)).astype(jnp.bfloat16)


def rotate(values, positions):
    half_dim = values.shape[-1] // 2
    frequency = rope_base ** (-(jnp.arange(half_dim, dtype=jnp.float32) * 2.0 / values.shape[-1]))
    angles = positions.astype(jnp.float32)[:, None, None] * frequency
    cosine = jnp.cos(angles)
    sine_part = jnp.sin(angles)
    lower_half = values[..., :half_dim]
    upper_half = values[..., half_dim:]
    return jnp.concatenate(
        [
            lower_half * cosine - upper_half * sine_part,
            upper_half * cosine + lower_half * sine_part,
        ],
        axis=-1,
    )


def lookup(table, indices):
    table_match = indices[..., None] == jnp.arange(table.shape[0], dtype=jnp.int32)
    return jnp.sum(jnp.where(table_match, table, 0), axis=-1)


def fold_rows(normed, first_weight, second_weight):
    return (
        jnp.dot(
            normed,
            lax.all_gather(first_weight, "wide", axis=0, tiled=True),
            preferred_element_type=jnp.float32,
        ),
        jnp.dot(
            normed,
            lax.all_gather(second_weight, "wide", axis=0, tiled=True),
            preferred_element_type=jnp.float32,
        ),
    )


def column_terms(left_rows, weight_block):
    return jnp.dot(
        left_rows,
        lax.all_gather(weight_block, "wide", axis=1, tiled=True),
        preferred_element_type=jnp.float32,
    )


def keyval_block(w_keyval, b_keyval, head_pair):
    pair_width = 2 * HD
    pair_offset = head_pair * pair_width
    return (w_keyval, b_keyval, pair_offset)


def add_branch(partial_terms, base_rows, narrow_index):
    share_sum = lax.psum_scatter(
        partial_terms.astype(jnp.bfloat16), "narrow", scatter_dimension=1, tiled=True
    ).astype(jnp.float32)
    share_width = share_sum.shape[1]
    base_share = lax.dynamic_slice_in_dim(base_rows, narrow_index * share_width, share_width, 1)
    updated = (base_share.astype(jnp.float32) + share_sum).astype(jnp.bfloat16)
    result_rows = lax.all_gather(updated, "narrow", axis=1, tiled=True)
    return result_rows


def attend(queries, keys_all, values_all, segment_ids, seg_offsets, row_base):
    tok_rows = queries.shape[0]
    local_heads = queries.shape[1] // HD
    total_rows = keys_all.shape[0]
    key_block = math.gcd(total_rows, 512)
    score_scale = HD ** (-0.5)
    stacked = (
        queries.reshape(tok_rows, local_heads, HD)
        .transpose(1, 0, 2)
        .reshape(local_heads * tok_rows, HD)
    )
    query_pos = row_base + jnp.arange(tok_rows, dtype=jnp.int32)
    query_pos_all = jnp.tile(query_pos, local_heads)
    query_seg_all = jnp.tile(segment_ids, local_heads)
    lowest = lookup(seg_offsets, segment_ids[:1])[0]
    first_block = lowest // key_block
    last_block = (row_base + tok_rows - 1) // key_block

    def visit_block(block_number, state_now):
        running_max, running_sum, accumulated = state_now
        key_start = block_number * key_block
        keys_here = lax.dynamic_slice_in_dim(keys_all, key_start, key_block, 0)
        values_here = lax.dynamic_slice_in_dim(values_all, key_start, key_block, 0)
        key_pos = key_start + jnp.arange(key_block, dtype=jnp.int32)
        key_seg = jnp.sum((key_pos[:, None] >= seg_offsets[None, 1:]).astype(jnp.int32), axis=1)
        visible = (
            (key_seg[None, :] == query_seg_all[:, None])
            & (key_pos[None, :] <= query_pos_all[:, None])
            & (key_pos[None, :] >= 0)
        )
        scores = (
            jnp.einsum("qd,kd->qk", stacked, keys_here, preferred_element_type=jnp.float32)
            * score_scale
        )
        scores = jnp.where(visible, scores, masked_score)
        new_max = jnp.maximum(running_max, jnp.max(scores, axis=1))
        weights = jnp.where(visible, jnp.exp(scores - new_max[:, None]), 0.0)
        factor = jnp.exp(running_max - new_max)
        running_sum = running_sum * factor + jnp.sum(weights, axis=1)
        accumulated = accumulated * factor[:, None] + jnp.dot(
            weights.astype(jnp.bfloat16), values_here, preferred_element_type=jnp.float32
        )
        return (new_max, running_sum, accumulated)

    row_count = stacked.shape[0]
    initial = (
        jnp.full((row_count,), masked_score, jnp.float32),
        jnp.zeros((row_count,), jnp.float32),
        jnp.zeros((row_count, HD), jnp.float32),
    )
    final_max, final_sum, accumulated = lax.fori_loop(
        first_block, last_block + 1, visit_block, initial
    )
    mixed_heads = (
        (accumulated / final_sum[:, None]).reshape(local_heads, tok_rows, HD).transpose(1, 0, 2)
    )
    return mixed_heads.reshape(tok_rows, local_heads * HD).astype(jnp.bfloat16)


def fill_pages(source, seg_lengths, seg_offsets, block_table, first_page, page_count):
    pages_here = first_page + jnp.arange(page_count, dtype=jnp.int32)
    page_match = block_table[None, :, :] == pages_here[:, None, None]
    seg_grid = jnp.arange(block_table.shape[0], dtype=jnp.int32)[None, :, None]
    page_grid = jnp.arange(block_table.shape[1], dtype=jnp.int32)[None, None, :]
    page_owner = jnp.sum(jnp.where(page_match, seg_grid, 0), axis=(1, 2))
    logical = jnp.sum(jnp.where(page_match, page_grid, 0), axis=(1, 2))
    in_use = jnp.any(page_match, axis=(1, 2))
    first_token = lookup(seg_offsets, page_owner) + logical * PAGE_LEN
    filled = lookup(seg_lengths, page_owner) - logical * PAGE_LEN
    slot_index = jnp.arange(PAGE_LEN, dtype=jnp.int32)
    row_ids = jnp.clip(first_token[:, None] + slot_index[None, :], 0, source.shape[0] - 1)
    keep_slot = in_use[:, None] & (slot_index[None, :] < filled[:, None])
    taken_rows = jnp.take(source, row_ids.reshape(-1), axis=0).reshape(
        page_count, PAGE_LEN, source.shape[1]
    )
    return jnp.where(keep_slot[:, :, None], taken_rows, jnp.zeros((), source.dtype))


def local(
    hidden_in,
    segment_ids,
    seg_lengths,
    seg_offsets,
    block_table,
    attn_gain,
    w_query,
    b_query,
    w_keyval,
    b_keyval,
    w_out,
    mlp_gain,
    w_gate,
    w_up,
    w_down,
    next_gain,
    w_query2,
    b_query2,
    w_keyval2,
    b_keyval2,
):
    tok_rows = hidden_in.shape[0]
    wide_index = lax.axis_index("wide")
    narrow_index = lax.axis_index("narrow")
    head_pair = narrow_index // 2
    kind_index = narrow_index % 2
    row_base = wide_index * tok_rows
    positions = row_base + jnp.arange(tok_rows, dtype=jnp.int32) - lookup(seg_offsets, segment_ids)
    normed = rms_norm(hidden_in, attn_gain)
    kv_weight, kv_bias, pair_offset = keyval_block(w_keyval, b_keyval, head_pair)
    query_sum, keyval_sum = fold_rows(normed, w_query, kv_weight)
    queries = query_sum + b_query.astype(jnp.float32)
    local_heads = queries.shape[1] // HD
    queries = (
        rotate(queries.reshape(tok_rows, local_heads, HD), positions)
        .reshape(tok_rows, local_heads * HD)
        .astype(jnp.bfloat16)
    )
    keyvals = (keyval_sum + kv_bias.astype(jnp.float32)).reshape(tok_rows, -1, 2, HD)
    keyvals = jnp.stack([rotate(keyvals[:, :, 0, :], positions), keyvals[:, :, 1, :]], axis=2)
    keyvals = keyvals.reshape(tok_rows, kv_weight.shape[1]).astype(jnp.bfloat16)
    gathered = lax.all_gather(keyvals, "wide", axis=0, tiled=True)
    source = lax.dynamic_slice_in_dim(gathered, pair_offset + kind_index * HD, HD, 1)
    keys_all = lax.dynamic_slice_in_dim(gathered, pair_offset, HD, 1)
    values_all = lax.dynamic_slice_in_dim(gathered, pair_offset + HD, HD, 1)
    mixed_heads = attend(queries, keys_all, values_all, segment_ids, seg_offsets, row_base)
    residual = add_branch(column_terms(mixed_heads, w_out), hidden_in, narrow_index)
    normed_mlp = rms_norm(residual, mlp_gain)
    gate_sum, up_sum = fold_rows(normed_mlp, w_gate, w_up)
    hidden_units = (jax.nn.silu(gate_sum) * up_sum).astype(jnp.bfloat16)
    hidden_out = add_branch(column_terms(hidden_units, w_down), residual, narrow_index)
    normed_next = rms_norm(hidden_out, next_gain)
    kv_weight_next, kv_bias_next, pair_offset_next = keyval_block(w_keyval2, b_keyval2, head_pair)
    query_next, keyval_next = fold_rows(normed_next, w_query2, kv_weight_next)
    next_query = (query_next + b_query2.astype(jnp.float32)).astype(jnp.bfloat16)
    keyval_next = keyval_next + kv_bias_next.astype(jnp.float32)
    next_keyval = lax.dynamic_slice_in_dim(
        keyval_next, pair_offset_next + kind_index * HD, HD, 1
    ).astype(jnp.bfloat16)
    page_count = tok_rows // PAGE_LEN + 1
    cache_block = fill_pages(
        source, seg_lengths, seg_offsets, block_table, wide_index * page_count, page_count
    )
    return (hidden_out, next_query, next_keyval, cache_block[None])


def solution(mesh):
    placed = (
        P("wide", None),
        P("wide"),
        P(),
        P(),
        P(),
        P(),
        P("wide", "narrow"),
        P("narrow"),
        P("wide", None),
        P(),
        P("narrow", "wide"),
        P(),
        P("wide", "narrow"),
        P("wide", "narrow"),
        P("narrow", "wide"),
        P(),
        P("wide", "narrow"),
        P("narrow"),
        P("wide", None),
        P(),
    )
    return jax.shard_map(
        local,
        mesh=mesh,
        in_specs=placed,
        out_specs=(
            P("wide", None),
            P("wide", "narrow"),
            P("wide", "narrow"),
            P("narrow", "wide", None, None),
        ),
        check_vma=False,
    )
```

profile of v0, /device:TPU:0, one launch (start us, length us, event | category | flops | bytes accessed | tf_op | source)
XLA Modules:
  0.0 521.2 jit_solution(14658357420002267087)
XLA Ops:
  7.2 0.7 all-gather.12.cloned.1.call-update
  7.9 0.7 all-gather.16.cloned.1.call-update
  8.7 0.7 convert_element_type.106
  9.4 0.7 convert_element_type.108
  10.1 0.8 select_reduce_fusion
  10.9 1.8 fusion.17
  12.7 0.5 multiply_cosine_fusion
  13.2 25.1 %all-gather.12.cloned.1.call-done = bf16[1536,512]{1,0:T(8,128)(2,1)} async-done(((bf16[192,512]{1,0:T(8,128)(2,1)}), bf16[1536,512]{1,0:T(8,128)(2,1)}) %all-gather.12.cloned.1.call-update) | async-done | bytes 1572880 | tf_op jit(solution)/shard_map/all_gather | solution.py:51
  38.3 3.0 convolution_add_fusion.1
  41.4 0.1 subtract_convert_fusion.1
  41.6 1.0 copy.42
  42.7 0.5 all-gather.18.cloned.1.call-update
  43.3 0.5 slice.25
  43.8 1.3 fusion.44
  47.8 16.5 %all-gather.16.cloned.1.call-done = bf16[1536,384]{1,0:T(8,128)(2,1)} async-done(((bf16[192,384]{1,0:T(8,128)(2,1)}), bf16[1536,384]{1,0:T(8,128)(2,1)}) %all-gather.16.cloned.1.call-update) | async-done | bytes 1179664 | tf_op jit(solution)/shard_map/all_gather | solution.py:46
  64.3 2.2 convolution_add_fusion.3
  66.5 0.1 subtract_convert_fusion
  66.7 0.2 copy.40
  66.9 36.6 %all-gather.14.cloned.1.call-done = bf16[4096,512]{1,0:T(8,128)(2,1)} async-done(((bf16[512,512]{1,0:T(8,128)(2,1)}), bf16[4096,512]{1,0:T(8,128)(2,1)}) %all-gather.14.cloned.1.call-update) | async-done | bytes 4194320 | tf_op jit(solution)/shard_map/all_gather | solution.py:202
  103.5 3.1 constant_dynamic-slice_fusion
  106.6 5.7 %while.15 = (s32[]{:T(128)}, f32[1536]{0:T(1024)S(1)}, f32[1536]{0:T(1024)S(1)}, f32[1536,128]{1,0:T(8,128)S(1)}, s32[]{:T(128)}, /*index=5*/s32[8]{0:T(128)S(1)...) while((s32[]{:T(128)}, f32[1536]{0:T(1024)S(1)}, ...), condition=%wide.region_7.8_spmd.clone, body=%wide.region_3.7_spmd.clone.sunk | while | flops 419576320 | bytes 11870495 | solution.py:132
  106.8 0.1 convert_reduce_fusion.2
  106.9 2.2 fusion.73
  109.1 1.4 fusion.74
  110.5 1.8 convolution_add_fusion.5
  112.4 0.3 divide_convert_fusion
  112.7 0.2 copy.41
  112.8 16.5 %all-gather.18.cloned.1.call-done = bf16[384,1536]{0,1:T(8,128)(2,1)} async-done(((bf16[384,192]{0,1:T(8,128)(2,1)}), bf16[384,1536]{0,1:T(8,128)(2,1)}) %all-gather.18.cloned.1.call-update) | async-done | bytes 1179664 | tf_op jit(solution)/shard_map/all_gather | solution.py:60
  129.3 2.3 convolution_convert_fusion.1
  131.6 1.6 copy.43
  133.3 41.8 %reduce-scatter.7.cloned.1.call-done = bf16[384,512]{1,0:T(8,128)(2,1)} async-done(((bf16[1536,512]{1,0:T(8,128)(2,1)}), bf16[384,512]{1,0:T(8,128)(2,1)}) %reduce-scatter.7.cloned.1.call-update) | async-done | bytes 393232
  175.1 1.2 copy.44
  176.3 1.8 add_convert_fusion.1
  178.3 0.7 all-gather.22.cloned.1.call-update
  179.0 0.7 all-gather.24.cloned.1.call-update
  179.8 0.7 all-gather.26.cloned.1.call-update
  180.5 0.2 reduce-scatter.9.cloned.1.call-start
  180.7 33.7 %all-gather.20.cloned.1.call-done = bf16[512,1536]{1,0:T(8,128)(2,1)} async-done(((bf16[512,384]{1,0:T(8,128)(2,1)}), bf16[512,1536]{1,0:T(8,128)(2,1)}) %all-gather.20.cloned.1.call-update) | async-done | bytes 1572880 | tf_op jit(solution)/shard_map/all_gather | solution.py:78
  214.4 1.8 fusion.20
  216.2 47.9 %all-gather.22.cloned.1.call-done = bf16[1536,2240]{1,0:T(8,128)(2,1)} async-done(((bf16[192,2240]{1,0:T(8,128)(2,1)}), bf16[1536,2240]{1,0:T(8,128)(2,1)}) %all-gather.22.cloned.1.call-update) | async-done | bytes 6881296 | tf_op jit(solution)/shard_map/all_gather | solution.py:46
  264.2 9.5 %fusion.28 = f32[512,2240]{0,1:T(8,128)} fusion(bf16[1536,2240]{1,0:T(8,128)(2,1)} %all-gather.22.cloned.1.call-done, bf16[512,1536]{1,0:T(8,128)(2,1)} %all-gather.20.cloned.1.call-done, f32[1536]{0:T(1024)S(1)} %convert_element_type.121, f32[512]{0:T(512)S(1)} %add_rsqrt_fusion.1), kind=kOutput, calls=%fused_computation.52 | convolution fusion | flops 3526361088 | bytes 13049856 | tf_op jit(solution)/shard_map/dot_general | solution.py:44
  273.6 41.3 %all-gather.24.cloned.1.call-done = bf16[1536,2240]{1,0:T(8,128)(2,1)} async-done(((bf16[192,2240]{1,0:T(8,128)(2,1)}), bf16[1536,2240]{1,0:T(8,128)(2,1)}) %all-gather.24.cloned.1.call-update) | async-done | bytes 6881296 | tf_op jit(solution)/shard_map/all_gather | solution.py:51
  314.9 50.8 %all-gather.26.cloned.1.call-done = bf16[2240,1536]{0,1:T(8,128)(2,1)} async-done(((bf16[2240,192]{0,1:T(8,128)(2,1)}), bf16[2240,1536]{0,1:T(8,128)(2,1)}) %all-gather.26.cloned.1.call-update) | async-done | bytes 6881296 | tf_op jit(solution)/shard_map/all_gather | solution.py:60
  365.7 15.9 %convolution_convert_fusion = bf16[512,1536]{1,0:T(8,128)(2,1)} fusion(bf16[2240,1536]{0,1:T(8,128)(2,1)} %all-gather.26.cloned.1.call-done, bf16[1536,2240]{1,0:T(8,128)(2,1)} %all-gather.24.cloned.1.call-done, f32[512,2240]{0,1:T(8,128)} %fusion.28, bf16[512,1536]{1,0:T(8,128)(2,1)S(1)} %copy-done.2, f32[1536]{0:T(1024)S(1)} %convert_element_type.121, ...), kind=kOutput, calls=%fused_computation.40 | convolution fusion | flops 7057244160 | bytes 21504000 | tf_op jit(solution)/shard_map/dot_general | solution.py:58
  381.6 2.7 copy.45
  384.4 35.4 %reduce-scatter.9.cloned.1.call-done = bf16[384,512]{1,0:T(8,128)(2,1)} async-done(((bf16[1536,512]{1,0:T(8,128)(2,1)}), bf16[384,512]{1,0:T(8,128)(2,1)}) %reduce-scatter.9.cloned.1.call-update) | async-done | bytes 393232
  419.8 1.2 copy.46
  421.0 0.8 add_convert_fusion
  421.9 0.5 all-gather.32.cloned.1.call-update
  422.5 0.7 all-gather.30.cloned.1.call-update
  423.2 0.3 fusion.37
  423.6 0.2 select_reduce_fusion.2
  424.0 0.3 compare_reduce_fusion
  424.2 0.1 fusion.41
  424.3 2.0 gather_fusion
  426.3 0.9 select_select_fusion
  427.2 30.9 %all-gather.28.cloned.1.call-done = bf16[512,1536]{1,0:T(8,128)(2,1)} async-done(((bf16[512,384]{1,0:T(8,128)(2,1)}), bf16[512,1536]{1,0:T(8,128)(2,1)}) %all-gather.28.cloned.1.call-update) | async-done | bytes 1572880 | tf_op jit(solution)/shard_map/all_gather | solution.py:78
  458.1 1.8 fusion.23
  459.9 24.6 %all-gather.32.cloned.1.call-done = bf16[1536,512]{1,0:T(8,128)(2,1)} async-done(((bf16[192,512]{1,0:T(8,128)(2,1)}), bf16[1536,512]{1,0:T(8,128)(2,1)}) %all-gather.32.cloned.1.call-update) | async-done | bytes 1572880 | tf_op jit(solution)/shard_map/all_gather | solution.py:51
  484.5 2.9 fusion.30
  487.4 0.7 fusion.35
  488.1 22.4 %all-gather.30.cloned.1.call-done = bf16[1536,384]{1,0:T(8,128)(2,1)} async-done(((bf16[192,384]{1,0:T(8,128)(2,1)}), bf16[1536,384]{1,0:T(8,128)(2,1)}) %all-gather.30.cloned.1.call-update) | async-done | bytes 1179664 | tf_op jit(solution)/shard_map/all_gather | solution.py:46
  510.5 3.0 fusion.26
  513.5 1.1 copy.63
  (75 shorter events, 1.2 us)
Async XLA Ops:
  7.2 31.1 %all-gather.12.cloned.1.call-start = ((), (), s32[]{:S(2)}) async-start(), calls=%async_computation.2 | async-start | bytes 1769472 | tf_op jit(solution)/shard_map/all_gather | solution.py:51
  7.9 56.4 %all-gather.16.cloned.1.call-start = ((), (), s32[]{:S(2)}) async-start(), calls=%async_computation.4 | async-start | bytes 1327104 | tf_op jit(solution)/shard_map/all_gather | solution.py:46
  8.6 94.9 %all-gather.14.cloned.1.call-start = ((), (), s32[]{:S(2)}) async-start(), calls=%async_computation.3 | async-start | bytes 4718592 | tf_op jit(solution)/shard_map/all_gather | solution.py:202
  41.3 2.0 copy-start.3
  41.3 2.5 copy-start.7
  41.3 6.4 %copy-start.8 = (bf16[384]{0:T(512)(128)(2,1)S(1)}, bf16[384]{0:T(512)(128)(2,1)}, u32[]{:S(2)}) copy-start(bf16[384]{0:T(512)(128)(2,1)} %param.29) | copy-start | bytes 2308
  41.3 22.9 %copy-start.1 = (bf16[512,1536]{1,0:T(8,128)(2,1)S(1)}, bf16[512,1536]{1,0:T(8,128)(2,1)}, u32[]{:S(2)}) copy-start(bf16[512,1536]{1,0:T(8,128)(2,1)} %param.22) | copy-start | bytes 4718596
  42.7 86.7 %all-gather.18.cloned.1.call-start = ((), (), s32[]{:S(2)}) async-start(), calls=%async_computation.5 | async-start | bytes 1327104 | tf_op jit(solution)/shard_map/all_gather | solution.py:60
  43.2 131.9 %reduce-scatter.7.cloned.1.call-start = ((), (), s32[]{:S(2)}) async-start(), calls=%async_computation.13 | async-start | bytes 1966080
  133.2 47.5 %copy-start.5 = (bf16[1536]{0:T(1024)(128)(2,1)S(1)}, bf16[1536]{0:T(1024)(128)(2,1)}, u32[]{:S(2)}) copy-start(bf16[1536]{0:T(1024)(128)(2,1)} %param.33) | copy-start | bytes 9220
  133.3 81.2 %all-gather.20.cloned.1.call-start = ((), (), s32[]{:S(2)}) async-start(), calls=%async_computation.6 | async-start | bytes 1966080 | tf_op jit(solution)/shard_map/all_gather | solution.py:78
  178.2 85.9 %all-gather.22.cloned.1.call-start = ((), (), s32[]{:S(2)}) async-start(), calls=%async_computation.7 | async-start | bytes 7962624 | tf_op jit(solution)/shard_map/all_gather | solution.py:46
  179.0 136.0 %all-gather.24.cloned.1.call-start = ((), (), s32[]{:S(2)}) async-start(), calls=%async_computation.8 | async-start | bytes 7962624 | tf_op jit(solution)/shard_map/all_gather | solution.py:51
  179.7 186.0 %all-gather.26.cloned.1.call-start = ((), (), s32[]{:S(2)}) async-start(), calls=%async_computation.9 | async-start | bytes 7962624 | tf_op jit(solution)/shard_map/all_gather | solution.py:60
  180.5 239.3 %reduce-scatter.9.cloned.1.call-start = ((), (), s32[]{:S(2)}) async-start(), calls=%async_computation.14 | async-start | bytes 1966080
  216.2 149.5 %copy-start.2 = (bf16[512,1536]{1,0:T(8,128)(2,1)S(1)}, bf16[512,1536]{1,0:T(8,128)(2,1)}, u32[]{:S(2)}) copy-start(bf16[512,1536]{1,0:T(8,128)(2,1)} %all-gather.20.cloned.1.call-done) | copy-start | bytes 4718596
  381.6 41.6 %copy-start.4 = (s32[8,16]{1,0:T(8,128)S(1)}, s32[8,16]{1,0:T(8,128)}, u32[]{:S(2)}) copy-start(s32[8,16]{1,0:T(8,128)} %param.26) | copy-start | bytes 1540
  381.6 42.0 %copy-start.10 = (s32[8]{0:T(128)S(1)}, s32[8]{0:T(128)}, u32[]{:S(2)}) copy-start(s32[8]{0:T(128)} %param.24) | copy-start | bytes 100
  381.6 42.2 %copy-start.6 = (bf16[1536]{0:T(1024)(128)(2,1)S(1)}, bf16[1536]{0:T(1024)(128)(2,1)}, u32[]{:S(2)}) copy-start(bf16[1536]{0:T(1024)(128)(2,1)} %param.37) | copy-start | bytes 9220
  381.6 42.2 %copy-start.11 = (bf16[512]{0:T(512)(128)(2,1)S(1)}, bf16[512]{0:T(512)(128)(2,1)}, u32[]{:S(2)}) copy-start(bf16[512]{0:T(512)(128)(2,1)} %param.41) | copy-start | bytes 3076
  381.6 42.3 %copy-start.9 = (bf16[384]{0:T(512)(128)(2,1)S(1)}, bf16[384]{0:T(512)(128)(2,1)}, u32[]{:S(2)}) copy-start(bf16[384]{0:T(512)(128)(2,1)} %param.39) | copy-start | bytes 2308
  384.3 73.8 %all-gather.28.cloned.1.call-start = ((), (), s32[]{:S(2)}) async-start(), calls=%async_computation.10 | async-start | bytes 1966080 | tf_op jit(solution)/shard_map/all_gather | solution.py:78
  421.9 62.7 %all-gather.32.cloned.1.call-start = ((), (), s32[]{:S(2)}) async-start(), calls=%async_computation.12 | async-start | bytes 1769472 | tf_op jit(solution)/shard_map/all_gather | solution.py:51
  422.4 88.1 %all-gather.30.cloned.1.call-start = ((), (), s32[]{:S(2)}) async-start(), calls=%async_computation.11 | async-start | bytes 1327104 | tf_op jit(solution)/shard_map/all_gather | solution.py:46
  459.9 50.6 %copy-start = (bf16[512,1536]{1,0:T(8,128)(2,1)S(1)}, bf16[512,1536]{1,0:T(8,128)(2,1)}, u32[]{:S(2)}) copy-start(bf16[512,1536]{1,0:T(8,128)(2,1)} %all-gather.28.cloned.1.call-done) | copy-start | bytes 4718596
Sparse Core Ops, SparseCore 0:
  9.9 28.3 all-gather.11
  40.2 24.0 all-gather.15
  66.8 36.7 all-gather.13
  105.2 24.0 all-gather.17
  133.4 41.7 reduce-scatter.6
  178.3 36.0 all-gather.19
  216.3 47.7 all-gather.21
  266.0 48.8 all-gather.23
  316.8 48.8 all-gather.25
  384.5 35.2 reduce-scatter.8
  422.0 36.0 all-gather.27
  459.8 24.6 all-gather.31
  486.4 24.0 all-gather.29
where the time goes:
time: 522 us; the launch traced here: 521 us
  waiting for transfers between devices  429 us (82%)
  matrix products  42.8 us (8%)
  between operations  16.9 us (3%)
  other arithmetic  16.8 us (3%)
  local copies, waits for them, and re-layouts  15.1 us (3%)
    all_gather x3, waiting for transfers between devices, fold_rows(): lax.all_gather(second_weight, 'wide', axis=0, tiled=True)  91 us
    all_gather x3, waiting for transfers between devices, fold_rows(): lax.all_gather(first_weight, 'wide', axis=0, tiled=True)  86.8 us
    unnamed x15, waiting for transfers between devices  82.5 us
    all_gather x2, waiting for transfers between devices, column_terms(): lax.all_gather(weight_block, 'wide', axis=1, tiled=True)  67.3 us
    all_gather x2, waiting for transfers between devices, add_branch(): result_rows = lax.all_gather(updated, 'narrow', axis=1, tiled=True)  64.6 us
    all_gather x1, waiting for transfers between devices, local(): gathered = lax.all_gather(keyvals, 'wide', axis=0, tiled=True)  36.6 us
    dot_general x2, matrix products, column_terms(): jnp.dot(left_rows, lax.all_gather(weight_block, 'wide', axis=1, tiled=Tru...  18.2 us
    dot_general x3, matrix products, fold_rows(): jnp.dot(normed, lax.all_gather(first_weight, 'wide', axis=0, tiled=True),...  14.7 us
  transfers between devices with their start and end apart: 13, of which 13 were waited for; matrix products, arithmetic and copies ran while one was open for 8% of the time, Pallas kernels for 0%

commit v1 on v0

--- a/solution.py
+++ b/solution.py
@@ -75,7 +75,14 @@
     share_width = share_sum.shape[1]
     base_share = lax.dynamic_slice_in_dim(base_rows, narrow_index * share_width, share_width, 1)
     updated = (base_share.astype(jnp.float32) + share_sum).astype(jnp.bfloat16)
-    result_rows = lax.all_gather(updated, "narrow", axis=1, tiled=True)
+    ring = [updated]
+    for hop in range(3):
+        ring.append(lax.ppermute(ring[-1], "narrow", [(dev, (dev + 1) % 4) for dev in range(4)]))
+    result_rows = jnp.roll(
+        jnp.concatenate(ring[::-1], axis=1),
+        (lax.axis_index("narrow") + 1) * ring[0].shape[1],
+        axis=1,
+    )
     return result_rows
 
 

time: 522 us -> 449 us (0.86)
  waiting for transfers between devices: 429 us -> 343 us
  other arithmetic: 16.8 us -> 22.5 us
    all_gather x2 -> x0, waiting for transfers between devices: 64.6 us -> none  [add_branch(): result_rows = lax.all_gather(updated, 'narrow', axis=1, tiled=True)]
    ppermute x0 -> x6, waiting for transfers between devices: none -> 60.5 us  [add_branch(): lax.ppermute(ring[-1], 'narrow', [(dev, (dev + 1) % 4) for dev in range(4)])]
    all_gather x3, waiting for transfers between devices: 86.8 us -> 31.6 us  [fold_rows(): lax.all_gather(first_weight, 'wide', axis=0, tiled=True)]
    all_gather x3, waiting for transfers between devices: 91 us -> 65 us  [fold_rows(): lax.all_gather(second_weight, 'wide', axis=0, tiled=True)]
    unnamed x15 -> x13, waiting for transfers between devices: 82.5 us -> 83.2 us
  transfers between devices with their start and end apart: 13 -> 17, of which waited for: 13 -> 16; matrix products, arithmetic and copies ran while one was open for 8% -> 13% of each run, Pallas kernels for 0% -> 0%
where the time goes in v1:
time: 449 us; the launch traced here: 448 us
  waiting for transfers between devices  343 us (76%)
  matrix products  45.2 us (10%)
  other arithmetic  22.5 us (5%)
  local copies, waits for them, and re-layouts  18.7 us (4%)
  between operations  16.9 us (4%)
    unnamed x13, waiting for transfers between devices  83.2 us
    all_gather x2, waiting for transfers between devices, column_terms(): lax.all_gather(weight_block, 'wide', axis=1, tiled=True)  65.8 us
    all_gather x3, waiting for transfers between devices, fold_rows(): lax.all_gather(second_weight, 'wide', axis=0, tiled=True)  65 us
    ppermute x6, waiting for transfers between devices, add_branch(): lax.ppermute(ring[-1], 'narrow', [(dev, (dev + 1) % 4) for dev in range(4)])  60.5 us
    all_gather x1, waiting for transfers between devices, local(): gathered = lax.all_gather(keyvals, 'wide', axis=0, tiled=True)  36.6 us
    all_gather x3, waiting for transfers between devices, fold_rows(): lax.all_gather(first_weight, 'wide', axis=0, tiled=True)  31.6 us
    dot_general x2, matrix products, column_terms(): jnp.dot(left_rows, lax.all_gather(weight_block, 'wide', axis=1, tiled=Tru...  18.3 us
    dot_general x3, matrix products, fold_rows(): jnp.dot(normed, lax.all_gather(first_weight, 'wide', axis=0, tiled=True),...  16.1 us
  transfers between devices with their start and end apart: 17, of which 16 were waited for; matrix products, arithmetic and copies ran while one was open for 13% of the time, Pallas kernels for 0%

profile of v1, /device:TPU:0, one launch (start us, length us, event | category | flops | bytes accessed | tf_op | source)
XLA Modules:
  0.0 447.5 jit_solution(9987532575233637468)
XLA Ops:
  7.2 0.7 all-gather.10.cloned.1.call-update
  7.9 0.7 all-gather.14.cloned.1.call-update
  8.7 0.7 convert_element_type.106
  9.4 0.7 convert_element_type.108
  10.1 0.8 select_reduce_fusion
  10.9 1.8 fusion.17
  12.7 0.5 multiply_cosine_fusion
  13.2 25.1 %all-gather.10.cloned.1.call-done = bf16[1536,512]{1,0:T(8,128)(2,1)} async-done(((bf16[192,512]{1,0:T(8,128)(2,1)}), bf16[1536,512]{1,0:T(8,128)(2,1)}) %all-gather.10.cloned.1.call-update) | async-done | bytes 1572880 | tf_op jit(solution)/shard_map/all_gather | solution.py:51
  38.3 3.0 convolution_add_fusion.1
  41.6 1.0 copy.42
  42.7 0.5 all-gather.16.cloned.1.call-update
  43.3 0.5 slice.25
  43.8 1.3 fusion.56
  47.8 16.5 %all-gather.14.cloned.1.call-done = bf16[1536,384]{1,0:T(8,128)(2,1)} async-done(((bf16[192,384]{1,0:T(8,128)(2,1)}), bf16[1536,384]{1,0:T(8,128)(2,1)}) %all-gather.14.cloned.1.call-update) | async-done | bytes 1179664 | tf_op jit(solution)/shard_map/all_gather | solution.py:46
  64.3 2.2 convolution_add_fusion.3
  66.9 36.6 %all-gather.12.cloned.1.call-done = bf16[4096,512]{1,0:T(8,128)(2,1)} async-done(((bf16[512,512]{1,0:T(8,128)(2,1)}), bf16[4096,512]{1,0:T(8,128)(2,1)}) %all-gather.12.cloned.1.call-update) | async-done | bytes 4194320 | tf_op jit(solution)/shard_map/all_gather | solution.py:209
  103.5 3.6 constant_dynamic-slice_fusion
  107.2 6.6 %while.15 = (s32[]{:T(128)}, f32[1536]{0:T(1024)S(1)}, f32[1536]{0:T(1024)S(1)}, f32[1536,128]{1,0:T(8,128)S(1)}, s32[]{:T(128)}, /*index=5*/s32[8]{0:T(128)S(1)...) while((s32[]{:T(128)}, f32[1536]{0:T(1024)S(1)}, ...), condition=%wide.region_7.8_spmd.clone, body=%wide.region_3.7_spmd.clone.sunk | while | flops 419576320 | bytes 11862303 | solution.py:139
  107.5 2.2 fusion.78
  109.7 1.4 fusion.79
  111.1 2.7 convolution_add_fusion.5
  114.3 15.0 %all-gather.16.cloned.1.call-done = bf16[384,1536]{0,1:T(8,128)(2,1)} async-done(((bf16[384,192]{0,1:T(8,128)(2,1)}), bf16[384,1536]{0,1:T(8,128)(2,1)}) %all-gather.16.cloned.1.call-update) | async-done | bytes 1179664 | tf_op jit(solution)/shard_map/all_gather | solution.py:60
  129.3 2.3 convolution_convert_fusion.1
  131.6 1.6 copy.43
  133.3 0.5 all-gather.18.cloned.1.call-update
  133.9 0.7 all-gather.20.cloned.1.call-update
  134.6 0.7 all-gather.22.cloned.1.call-update
  135.4 44.9 %reduce-scatter.7.cloned.1.call-done = bf16[384,512]{1,0:T(8,128)(2,1)} async-done(((bf16[1536,512]{1,0:T(8,128)(2,1)}), bf16[384,512]{1,0:T(8,128)(2,1)}) %reduce-scatter.7.cloned.1.call-update) | async-done | bytes 393232
  180.3 1.2 copy.44
  181.6 0.4 collective-permute-start
  182.0 12.1 %collective-permute-done = bf16[512,384]{1,0:T(8,128)(2,1)S(1)} collective-permute-done((bf16[512,384]{1,0:T(8,128)(2,1)S(1)}, bf16[512,384]{1,0:T(8,128)(2,1)S(1)}, u32[]{:S(2)}, u32[]{:S(2)}) %collective-permute-start) | collective-permute-done | bytes 393248 | tf_op jit(solution)/shard_map/ppermute | solution.py:80
  194.1 0.7 copy-done.2
  194.9 11.6 %collective-permute-done.1 = bf16[512,384]{1,0:T(8,128)(2,1)S(1)} collective-permute-done((bf16[512,384]{1,0:T(8,128)(2,1)S(1)}, bf16[512,384]{1,0:T(8,128)(2,1)S(1)}, u32[]{:S(2)}, u32[]{:S(2)}) %collective-permute-start.1) | collective-permute-done | bytes 393248 | tf_op jit(solution)/shard_map/ppermute | solution.py:80
  206.5 0.7 copy-done.3
  207.2 10.0 %collective-permute-done.2 = bf16[512,384]{1,0:T(8,128)(2,1)} collective-permute-done((bf16[512,384]{1,0:T(8,128)(2,1)S(1)}, bf16[512,384]{1,0:T(8,128)(2,1)}, u32[]{:S(2)}, u32[]{:S(2)}) %collective-permute-start.2) | collective-permute-done | bytes 393248 | tf_op jit(solution)/shard_map/ppermute | solution.py:80
  217.3 2.0 maximum_maximum_fusion
  219.3 1.3 fusion.20
  220.6 9.2 %all-gather.18.cloned.1.call-done = bf16[1536,2240]{1,0:T(8,128)(2,1)} async-done(((bf16[192,2240]{1,0:T(8,128)(2,1)}), bf16[1536,2240]{1,0:T(8,128)(2,1)}) %all-gather.18.cloned.1.call-update) | async-done | bytes 6881296 | tf_op jit(solution)/shard_map/all_gather | solution.py:46
  229.9 10.8 %fusion.40 = f32[512,2240]{0,1:T(8,128)} fusion(bf16[1536,2240]{1,0:T(8,128)(2,1)} %all-gather.18.cloned.1.call-done, f32[1536]{0:T(1024)S(1)} %convert_element_type.121, f32[512]{0:T(512)S(1)} %add_rsqrt_fusion.1, bf16[512,3072]{1,0:T(8,128)(2,1)S(1)} %maximum_maximum_fusion, s32[]{:T(128)S(6)} %select_n.139), kind=kOutput, calls=%fused_computation.72 | convolution fusion | flops 3526361088 | bytes 13051908 | tf_op jit(solution)/shard_map/dot_general | solution.py:44
  240.7 39.9 %all-gather.20.cloned.1.call-done = bf16[1536,2240]{1,0:T(8,128)(2,1)} async-done(((bf16[192,2240]{1,0:T(8,128)(2,1)}), bf16[1536,2240]{1,0:T(8,128)(2,1)}) %all-gather.20.cloned.1.call-update) | async-done | bytes 6881296 | tf_op jit(solution)/shard_map/all_gather | solution.py:51
  280.6 50.8 %all-gather.22.cloned.1.call-done = bf16[2240,1536]{0,1:T(8,128)(2,1)} async-done(((bf16[2240,192]{0,1:T(8,128)(2,1)}), bf16[2240,1536]{0,1:T(8,128)(2,1)}) %all-gather.22.cloned.1.call-update) | async-done | bytes 6881296 | tf_op jit(solution)/shard_map/all_gather | solution.py:60
  331.4 16.0 %convolution_convert_fusion = bf16[512,1536]{1,0:T(8,128)(2,1)} fusion(bf16[2240,1536]{0,1:T(8,128)(2,1)} %all-gather.22.cloned.1.call-done, bf16[1536,2240]{1,0:T(8,128)(2,1)} %all-gather.20.cloned.1.call-done, f32[512,2240]{0,1:T(8,128)} %fusion.40, f32[1536]{0:T(1024)S(1)} %convert_element_type.121, f32[512]{0:T(512)S(1)} %add_rsqrt_fusion.1, ...), kind=kOutput, calls=%fused_computation.49 | convolution fusion | flops 7057244160 | bytes 21506052 | tf_op jit(solution)/shard_map/dot_general | solution.py:58
  347.4 2.6 copy.45
  350.1 0.5 all-gather.26.cloned.1.call-update
  350.7 0.7 all-gather.24.cloned.1.call-update
  351.4 0.9 fusion.46
  352.3 33.3 %reduce-scatter.9.cloned.1.call-done = bf16[384,512]{1,0:T(8,128)(2,1)} async-done(((bf16[1536,512]{1,0:T(8,128)(2,1)}), bf16[384,512]{1,0:T(8,128)(2,1)}) %reduce-scatter.9.cloned.1.call-update) | async-done | bytes 393232
  385.5 1.9 copy.46
  387.5 1.2 add_convert_fusion
  388.7 0.4 collective-permute-start.3
  389.1 0.9 compare_reduce_fusion
  390.0 0.9 select_reduce_fusion.2
  390.9 10.3 %collective-permute-done.3 = bf16[512,384]{1,0:T(8,128)(2,1)S(1)} collective-permute-done((bf16[512,384]{1,0:T(8,128)(2,1)S(1)}, bf16[512,384]{1,0:T(8,128)(2,1)S(1)}, u32[]{:S(2)}, u32[]{:S(2)}) %collective-permute-start.3) | collective-permute-done | bytes 393248 | tf_op jit(solution)/shard_map/ppermute | solution.py:80
  401.4 11.4 %collective-permute-done.4 = bf16[512,384]{1,0:T(8,128)(2,1)S(1)} collective-permute-done((bf16[512,384]{1,0:T(8,128)(2,1)S(1)}, bf16[512,384]{1,0:T(8,128)(2,1)S(1)}, u32[]{:S(2)}, u32[]{:S(2)}) %collective-permute-start.4) | collective-permute-done | bytes 393248 | tf_op jit(solution)/shard_map/ppermute | solution.py:80
  412.8 0.8 dynamic-slice
  413.6 0.7 convert_element_type.130
  414.3 3.3 gather_fusion
  417.6 0.9 select_select_fusion
  418.5 5.0 %collective-permute-done.5 = bf16[512,384]{1,0:T(8,128)(2,1)S(1)} collective-permute-done((bf16[512,384]{1,0:T(8,128)(2,1)S(1)}, bf16[512,384]{1,0:T(8,128)(2,1)S(1)}, u32[]{:S(2)}, u32[]{:S(2)}) %collective-permute-start.5) | collective-permute-done | bytes 393248 | tf_op jit(solution)/shard_map/ppermute | solution.py:80
  423.5 4.8 %fusion.23 = (f32[512]{0:T(512)S(1)}, bf16[512,1536]{1,0:T(8,128)(2,1)S(1)}) fusion(s32[]{:T(128)S(6)} %select_n.139, bf16[512,384]{1,0:T(8,128)(2,1)S(1)} %add_convert_fusion, bf16[512,384]{1,0:T(8,128)(2,1)S(1)} %collective-permute-done.3, bf16[512,384]{1,0:T(8,128)(2,1)S(1)} %collective-permute-done.4, bf16[512,384]{1,0:T(8,128)(2,1)S(1)} %collective-permute-done.5), kind=kLoop, calls=%fused_computation.37 | loop fusion | flops 14941696 | bytes 3147780 | tf_op jit(solution)/shard_map/reduce_sum | solution.py:16
  428.4 3.0 fusion.34
  431.3 0.7 fusion.44
  432.0 5.9 %all-gather.24.cloned.1.call-done = bf16[1536,384]{1,0:T(8,128)(2,1)} async-done(((bf16[192,384]{1,0:T(8,128)(2,1)}), bf16[1536,384]{1,0:T(8,128)(2,1)}) %all-gather.24.cloned.1.call-update) | async-done | bytes 1179664 | tf_op jit(solution)/shard_map/all_gather | solution.py:46
  438.0 3.0 fusion.33
  (79 shorter events, 2.2 us)
Async XLA Ops:
  7.2 31.1 %all-gather.10.cloned.1.call-start = ((), (), s32[]{:S(2)}) async-start(), calls=%async_computation.2 | async-start | bytes 1769472 | tf_op jit(solution)/shard_map/all_gather | solution.py:51
  7.9 56.4 %all-gather.14.cloned.1.call-start = ((), (), s32[]{:S(2)}) async-start(), calls=%async_computation.4 | async-start | bytes 1327104 | tf_op jit(solution)/shard_map/all_gather | solution.py:46
  8.6 94.9 %all-gather.12.cloned.1.call-start = ((), (), s32[]{:S(2)}) async-start(), calls=%async_computation.3 | async-start | bytes 4718592 | tf_op jit(solution)/shard_map/all_gather | solution.py:209
  41.3 2.0 copy-start.4
  41.3 2.5 copy-start.8
  41.3 6.4 %copy-start.10 = (bf16[384]{0:T(512)(128)(2,1)S(1)}, bf16[384]{0:T(512)(128)(2,1)}, u32[]{:S(2)}) copy-start(bf16[384]{0:T(512)(128)(2,1)} %param.31) | copy-start | bytes 2308
  41.3 22.9 %copy-start = (bf16[512,1536]{1,0:T(8,128)(2,1)S(1)}, bf16[512,1536]{1,0:T(8,128)(2,1)}, u32[]{:S(2)}) copy-start(bf16[512,1536]{1,0:T(8,128)(2,1)} %param.24) | copy-start | bytes 4718596
  42.7 86.7 %all-gather.16.cloned.1.call-start = ((), (), s32[]{:S(2)}) async-start(), calls=%async_computation.5 | async-start | bytes 1327104 | tf_op jit(solution)/shard_map/all_gather | solution.py:60
  43.2 137.0 %reduce-scatter.7.cloned.1.call-start = ((), (), s32[]{:S(2)}) async-start(), calls=%async_computation.11 | async-start | bytes 1966080
  133.2 73.3 %copy-start.6 = (bf16[1536]{0:T(1024)(128)(2,1)S(1)}, bf16[1536]{0:T(1024)(128)(2,1)}, u32[]{:S(2)}) copy-start(bf16[1536]{0:T(1024)(128)(2,1)} %param.35) | copy-start | bytes 9220
  133.2 96.6 %all-gather.18.cloned.1.call-start = ((), (), s32[]{:S(2)}) async-start(), calls=%async_computation.6 | async-start | bytes 7962624 | tf_op jit(solution)/shard_map/all_gather | solution.py:46
  133.8 146.8 %all-gather.20.cloned.1.call-start = ((), (), s32[]{:S(2)}) async-start(), calls=%async_computation.7 | async-start | bytes 7962624 | tf_op jit(solution)/shard_map/all_gather | solution.py:51
  134.6 196.8 %all-gather.22.cloned.1.call-start = ((), (), s32[]{:S(2)}) async-start(), calls=%async_computation.8 | async-start | bytes 7962624 | tf_op jit(solution)/shard_map/all_gather | solution.py:60
  135.3 250.2 %reduce-scatter.9.cloned.1.call-start = ((), (), s32[]{:S(2)}) async-start(), calls=%async_computation.12 | async-start | bytes 1966080
  181.6 12.6 %collective-permute-start = (bf16[512,384]{1,0:T(8,128)(2,1)S(1)}, bf16[512,384]{1,0:T(8,128)(2,1)S(1)}, u32[]{:S(2)}, u32[]{:S(2)}) collective-permute-start(bf16[512,384]{1,0:T(8,128)(2,1)S(1)} %add_convert_fusion.1), channel_id=1, source_target_pairs={{0,1},{1,2},{2,3},{3,0},{4,5},{5,6},{6,7},{7,4},{8,9},{9,10},{10,1... | collective-permute-start | bytes 1179656 | tf_op jit(solution)/shard_map/ppermute | solution.py:80
  194.1 0.7 copy-start.2
  194.9 11.6 %collective-permute-start.1 = (bf16[512,384]{1,0:T(8,128)(2,1)S(1)}, bf16[512,384]{1,0:T(8,128)(2,1)S(1)}, u32[]{:S(2)}, u32[]{:S(2)}) collective-permute-start(bf16[512,384]{1,0:T(8,128)(2,1)S(1)} %collective-permute-done), channel_id=1, source_target_pairs={{0,1},{1,2},{2,3},{3,0},{4,5},{5,6},{6,7},{7,4},{8,9},{9,10},{10,1... | collective-permute-start | bytes 1179656 | tf_op jit(solution)/shard_map/ppermute | solution.py:80
  206.5 0.7 copy-start.3
  206.5 10.8 %collective-permute-start.2 = (bf16[512,384]{1,0:T(8,128)(2,1)S(1)}, bf16[512,384]{1,0:T(8,128)(2,1)}, u32[]{:S(2)}, u32[]{:S(2)}) collective-permute-start(bf16[512,384]{1,0:T(8,128)(2,1)S(1)} %collective-permute-done.1), channel_id=1, source_target_pairs={{0,1},{1,2},{2,3},{3,0},{4,5},{5,6},{6,7},{7,4},{8,9},{9,10},{10,1... | collective-permute-start | bytes 1179656 | tf_op jit(solution)/shard_map/ppermute | solution.py:80
  347.4 4.0 copy-start.5
  347.4 65.4 %copy-start.7 = (bf16[1536]{0:T(1024)(128)(2,1)S(1)}, bf16[1536]{0:T(1024)(128)(2,1)}, u32[]{:S(2)}) copy-start(bf16[1536]{0:T(1024)(128)(2,1)} %param.39) | copy-start | bytes 9220
  350.0 78.3 %all-gather.26.cloned.1.call-start = ((), (), s32[]{:S(2)}) async-start(), calls=%async_computation.10 | async-start | bytes 1769472 | tf_op jit(solution)/shard_map/all_gather | solution.py:51
  350.6 87.3 %all-gather.24.cloned.1.call-start = ((), (), s32[]{:S(2)}) async-start(), calls=%async_computation.9 | async-start | bytes 1327104 | tf_op jit(solution)/shard_map/all_gather | solution.py:46
  351.4 34.2 %copy-start.9 = (s32[5]{0:T(128)}, s32[5]{0:T(128)S(1)}, u32[]{:S(2)}) copy-start(s32[5]{0:T(128)S(1)} %iota_add_fusion.2) | copy-start | bytes 64
  388.7 12.5 %collective-permute-start.3 = (bf16[512,384]{1,0:T(8,128)(2,1)S(1)}, bf16[512,384]{1,0:T(8,128)(2,1)S(1)}, u32[]{:S(2)}, u32[]{:S(2)}) collective-permute-start(bf16[512,384]{1,0:T(8,128)(2,1)S(1)} %add_convert_fusion), channel_id=1, source_target_pairs={{0,1},{1,2},{2,3},{3,0},{4,5},{5,6},{6,7},{7,4},{8,9},{9,10},{10,1... | collective-permute-start | bytes 1179656 | tf_op jit(solution)/shard_map/ppermute | solution.py:80
  401.2 11.6 %collective-permute-start.4 = (bf16[512,384]{1,0:T(8,128)(2,1)S(1)}, bf16[512,384]{1,0:T(8,128)(2,1)S(1)}, u32[]{:S(2)}, u32[]{:S(2)}) collective-permute-start(bf16[512,384]{1,0:T(8,128)(2,1)S(1)} %collective-permute-done.3), channel_id=1, source_target_pairs={{0,1},{1,2},{2,3},{3,0},{4,5},{5,6},{6,7},{7,4},{8,9},{9,10},{10,1... | collective-permute-start | bytes 1179656 | tf_op jit(solution)/shard_map/ppermute | solution.py:80
  412.8 10.7 %collective-permute-start.5 = (bf16[512,384]{1,0:T(8,128)(2,1)S(1)}, bf16[512,384]{1,0:T(8,128)(2,1)S(1)}, u32[]{:S(2)}, u32[]{:S(2)}) collective-permute-start(bf16[512,384]{1,0:T(8,128)(2,1)S(1)} %collective-permute-done.4), channel_id=1, source_target_pairs={{0,1},{1,2},{2,3},{3,0},{4,5},{5,6},{6,7},{7,4},{8,9},{9,10},{10,1... | collective-permute-start | bytes 1179656 | tf_op jit(solution)/shard_map/ppermute | solution.py:80
  428.3 9.6 %copy-start.1 = (bf16[512,1536]{1,0:T(8,128)(2,1)}, bf16[512,1536]{1,0:T(8,128)(2,1)S(1)}, u32[]{:S(2)}) copy-start(bf16[512,1536]{1,0:T(8,128)(2,1)S(1)} %get-tuple-element.123) | copy-start | bytes 4718596
Sparse Core Ops, SparseCore 0:
  9.9 28.3 all-gather.9
  40.2 24.0 all-gather.13
  66.8 36.7 all-gather.11
  105.2 24.0 all-gather.15
  133.4 46.8 reduce-scatter.6
  182.0 47.8 all-gather.17
  231.7 48.8 all-gather.19
  282.5 48.8 all-gather.21
  350.2 35.3 reduce-scatter.8
  387.3 24.6 all-gather.25
  413.9 24.0 all-gather.23
